TPU v7x, 1024 devices: a whole 4x8x16 slice. The times are simulated.
1024 devices in a mesh: group: 4 (over z_hi), dp: 4 (over z_lo), mp: 64 (over y, x, core).
Axes of the slice: x: 4, y: 8, z: 16 (z_hi: 4, z_lo: 4; z = z_hi * 4 + z_lo), core: 2. Of those that a mesh axis runs over, the one named last changes fastest.
Arguments:
- patch_rows: bfloat16 [16, 128, 1280], P(('group', 'dp')), may hold values from -6 to 6
- ln_gain: float32 [1280], replicated, may hold values from 0.5 to 1.5
- ln_bias: float32 [1280], replicated, may hold values from -1.5 to 1.5
- merge_up: bfloat16 [5120, 5120], P(None, 'mp'), may hold values from -0.078125 to 0.078125
- merge_up_bias: float32 [5120], P('mp'), may hold values from -2.5 to 2.5
- merge_down: bfloat16 [5120, 8192], P('mp'), may hold values from -0.078125 to 0.078125
- merge_down_bias: float32 [8192], P('mp'), may hold values from -2.5 to 2.5
- row_owner: int32 [512, 1], replicated, may hold values from 0 to 15; in each aligned block of 32 rows (0 to 31, 32 to 63, ...) at most 4 rows name the same one
- text_embed: bfloat16 [16, 256, 8192], P(('group', 'dp')), may hold values from -6 to 6
- doc_ids: int32 [16, 256], P(('group', 'dp')), may hold values from 0 to 7, never falling along the last dimension, each value on 1 to 64 neighbouring positions
- rms_gain: float32 [8192], replicated, may hold values from 0.5 to 1.5
- w_query: bfloat16 [8192, 8192], P(None, 'mp')
- query_bias: float32 [8192], P('mp'), may hold values from -2.5 to 2.5
- w_keyval: bfloat16 [8192, 2, 1024], P(None, None, 'mp'), may hold values from -0.0625 to 0.0625
- keyval_bias: float32 [2, 1024], P(None, 'mp'), may hold values from -2.5 to 2.5
Outputs:
- attention: bfloat16 [16, 256, 8192], P(('group', 'dp'), None, 'mp')
Inputs may be any that keep to these rules, and one draw needn't show every extreme that they name: `row_owner`: in each aligned block of 32 rows (the rows of one image owner) no owner is named more than 4 times, a bound that some block reaches.
All inputs are finite; a program needn't handle non-finite values.
Results may differ from a plain program's by a relative error of at most 0.014.
The roundings to bfloat16 on the way count: a program that leaves them out, or rounds other values in their place, can miss the bound.
Values may be sent and summed in bfloat16 or wider, within the bound.
A program may use at most 64 MiB of HBM per device.

v0:
```python
import math

import jax
import jax.numpy as jnp
from jax import lax
from jax.sharding import PartitionSpec as P

HEADS = 64
KV_HEADS = 8
HEAD_DIM = 128


def per_device(
    patch_rows,
    ln_gain,
    ln_bias,
    merge_up,
    merge_up_bias,
    merge_down,
    merge_down_bias,
    row_owner,
    text_embed,
    doc_ids,
    rms_gain,
    w_query,
    query_bias,
    w_keyval,
    keyval_bias,
):
    owners = lax.axis_size(("group", "dp"))
    own_index = lax.axis_index(("group", "dp"))
    mp_index = lax.axis_index("mp")
    pixels = patch_rows[0].astype(jnp.float32)
    center = pixels - jnp.mean(pixels, axis=-1, keepdims=True)
    spread = jnp.mean(center * center, axis=-1, keepdims=True)
    normed_patch = (center * lax.rsqrt(spread + 1e-06) * ln_gain + ln_bias).astype(jnp.bfloat16)
    merged = normed_patch.reshape(-1, 4 * pixels.shape[1])
    merged_rows = merged.shape[0]
    hidden = jax.nn.gelu(
        jnp.dot(merged, merge_up, preferred_element_type=jnp.float32) + merge_up_bias,
        approximate=False,
    ).astype(jnp.bfloat16)
    partial_sum = jnp.dot(hidden, merge_down, preferred_element_type=jnp.float32)
    vision = (
        lax.psum_scatter(partial_sum, "mp", scatter_dimension=1, tiled=True) + merge_down_bias
    ).astype(jnp.bfloat16)
    col_width = vision.shape[1]
    capacity = max(2, 2 * merged_rows // owners)
    owner_all = row_owner[:, 0]
    owner_ids = jnp.arange(owners, dtype=jnp.int32)
    onehot = (owner_all[:, None] == owner_ids[None, :]).astype(jnp.int32)
    per_source = jnp.sum(onehot.reshape(owners, merged_rows, owners), axis=1)
    my_block = lax.dynamic_slice_in_dim(onehot, own_index * merged_rows, merged_rows, 0)
    block_rank = jnp.sum((jnp.cumsum(my_block, axis=0) - my_block) * my_block, axis=1)
    my_owner = jnp.sum(my_block * owner_ids[None, :], axis=1)
    slot_id = my_owner * capacity + block_rank
    all_slots = jnp.arange(owners * capacity, dtype=jnp.int32)
    select = (slot_id[:, None] == all_slots[None, :]).astype(jnp.bfloat16)
    outgoing = jnp.einsum("ms,mc->sc", select, vision, preferred_element_type=jnp.float32).astype(
        jnp.bfloat16
    )
    arrived = lax.all_to_all(
        outgoing.reshape(owners, capacity, col_width),
        ("group", "dp"),
        split_axis=0,
        concat_axis=0,
        tiled=True,
    )
    arrived = arrived.reshape(owners * capacity, col_width)
    incoming = lax.dynamic_slice_in_dim(per_source, own_index, 1, 1)[:, 0]
    offsets = jnp.cumsum(incoming) - incoming
    total = jnp.sum(incoming)
    slot_rank = jnp.arange(capacity, dtype=jnp.int32)
    target = jnp.where(
        slot_rank[None, :] < incoming[:, None], offsets[:, None] + slot_rank[None, :], -1
    ).reshape(-1)
    text_rows = text_embed[0]
    seq_len = text_rows.shape[0]
    positions = jnp.arange(seq_len, dtype=jnp.int32)
    source_slot = jnp.sum(
        jnp.where(target[:, None] == positions[None, :], all_slots[:, None], 0), axis=0
    )
    is_image = (positions < total)[:, None]
    text_cols = lax.dynamic_slice_in_dim(text_rows, mp_index * col_width, col_width, 1)
    own_cols = jnp.where(is_image, jnp.take(arrived, source_slot, axis=0), text_cols)
    sequence = lax.all_gather(own_cols, "mp", axis=1, tiled=True)
    seq_f = sequence.astype(jnp.float32)
    normed_seq = (
        seq_f * lax.rsqrt(jnp.mean(seq_f * seq_f, axis=-1, keepdims=True) + 1e-06) * rms_gain
    ).astype(jnp.bfloat16)
    queries = (
        jnp.dot(normed_seq, w_query, preferred_element_type=jnp.float32) + query_bias
    ).astype(jnp.bfloat16)
    keyval_local = (
        jnp.einsum("sd,dtc->stc", normed_seq, w_keyval, preferred_element_type=jnp.float32)
        + keyval_bias
    ).astype(jnp.bfloat16)
    keyval_full = lax.all_gather(keyval_local, "mp", axis=2, tiled=True)
    keyval_heads = jnp.transpose(keyval_full.reshape(seq_len, 2, HEAD_DIM, KV_HEADS), (0, 1, 3, 2))
    local_heads = queries.shape[1] // HEAD_DIM
    group_size = HEADS // KV_HEADS
    kv_index = (mp_index * local_heads + jnp.arange(local_heads, dtype=jnp.int32)) // group_size
    keys = jnp.take(keyval_heads[:, 0], kv_index, axis=1)
    values = jnp.take(keyval_heads[:, 1], kv_index, axis=1)
    query_heads = queries.reshape(seq_len, local_heads, HEAD_DIM)
    scores = jnp.einsum(
        "qhd,khd->hqk", query_heads, keys, preferred_element_type=jnp.float32
    ) / math.sqrt(HEAD_DIM)
    documents = doc_ids[0]
    allowed = (documents[:, None] == documents[None, :]) & (
        positions[None, :] <= positions[:, None]
    )
    scores = jnp.where(allowed[None], scores, jnp.float32(-1e30))
    highest = jnp.max(scores, axis=-1, keepdims=True)
    weights = jnp.exp(scores - highest)
    probs = (weights / jnp.sum(weights, axis=-1, keepdims=True)).astype(jnp.bfloat16)
    output = jnp.einsum("hqk,khd->qhd", probs, values, preferred_element_type=jnp.float32)
    return output.astype(jnp.bfloat16).reshape(1, seq_len, local_heads * HEAD_DIM)


def solution(mesh):
    in_specs = (
        P(("group", "dp"), None, None),
        P(),
        P(),
        P(None, "mp"),
        P("mp"),
        P("mp", None),
        P("mp"),
        P(),
        P(("group", "dp"), None, None),
        P(("group", "dp"), None),
        P(),
        P(None, "mp"),
        P("mp"),
        P(None, None, "mp"),
        P(None, "mp"),
    )
    out_specs = P(("group", "dp"), None, "mp")
    return jax.shard_map(
        per_device, mesh=mesh, in_specs=in_specs, out_specs=out_specs, check_vma=False
    )
```

profile of v0, /device:TPU:1, one launch (start us, length us, event | category | flops | bytes accessed | tf_op | source)
XLA Modules:
  0.0 406.4 jit_solution(1103738814319741835)
XLA Ops:
  6.5 0.0 reduce-scatter.2.cloned.1.call-start
  6.6 1.2 convert_reduce_fusion
  7.8 1.2 fusion.18
  9.0 0.1 div.40
  9.1 2.0 reshape.218
  11.2 0.1 rsqrt.20
  11.3 0.2 mul.99
  11.4 0.1 copy.22
  11.6 0.1 sub.37
  11.7 0.1 copy.21
  12.0 3.5 fusion.46
  15.5 0.0 reduce-scatter.2.cloned.1.call-update
  15.5 0.1 dynamic-slice.8
  15.6 0.1 fusion.44
  15.7 0.1 reduce_window_sum.18
  15.8 0.5 broadcast.202
  16.3 0.7 reduce.12
  16.9 0.1 eq.65
  17.0 0.3 convert_reduce_fusion.1
  17.4 0.1 constant_dynamic-slice_fusion
  17.5 0.7 fusion.114
  18.2 0.1 add_select_fusion
  18.3 0.1 select_n.74
  18.4 0.1 select_reduce_fusion
  18.5 0.2 multiply_reduce_fusion
  18.7 0.7 compare_and_fusion
  19.3 164.4 %reduce-scatter.2.cloned.1.call-done = f32[32,128]{1,0:T(8,128)} async-done(((f32[32,8192]{1,0:T(8,128)}), f32[32,128]{1,0:T(8,128)}) %reduce-scatter.2.cloned.1.call-update) | async-done | bytes 16400 | tf_op jit(solution)/shard_map/reduce_scatter | solution.py:45
  183.7 1.6 convolution_convert_fusion.1
  185.3 12.8 %all-to-all-start = ((bf16[16,4,128]{2,1,0:T(4,128)(2,1)}), bf16[16,4,128]{2,1,0:T(4,128)(2,1)S(1)}, u32[]{:S(2)}, u32[]{:S(2)}) async-start(bf16[16,4,128]{2,1,0:T(4,128)(2,1)} %bitcast.4), calls=%async_computation.1 | async-start | bytes 32768 | tf_op jit(solution)/shard_map/all_to_all | solution.py:62
  198.1 0.0 all-gather.3.cloned.1.call-start
  198.1 11.3 %all-to-all-done = bf16[16,4,128]{2,1,0:T(4,128)(2,1)S(1)} async-done(((bf16[16,4,128]{2,1,0:T(4,128)(2,1)}), bf16[16,4,128]{2,1,0:T(4,128)(2,1)S(1)}, u32[]{:S(2)}, u32[]{:S(2)}) %all-to-all-start) | async-done | bytes 16416 | tf_op jit(solution)/shard_map/all_to_all | solution.py:62
  209.4 0.9 gather_fusion
  210.3 1.6 bitcast_select_fusion
  211.9 0.0 all-gather.3.cloned.1.call-update
  211.9 0.0 all-gather.5.cloned.1.call-start
  212.0 87.5 %all-gather.3.cloned.1.call-done = bf16[256,8192]{1,0:T(8,128)(2,1)} async-done(((bf16[256,128]{1,0:T(8,128)(2,1)}), bf16[256,8192]{1,0:T(8,128)(2,1)}) %all-gather.3.cloned.1.call-update) | async-done | bytes 4194320 | tf_op jit(solution)/shard_map/all_gather | solution.py:86
  299.5 3.3 fusion
  302.8 0.2 copy-done.1
  303.0 1.4 fusion.5
  304.4 0.7 add_convert_fusion.2
  305.1 0.0 all-gather.5.cloned.1.call-update
  305.1 86.1 %all-gather.5.cloned.1.call-done = bf16[256,2,1024]{0,2,1:T(8,128)(2,1)} async-done(((bf16[256,2,16]{0,2,1:T(8,128)(2,1)}), bf16[256,2,1024]{0,2,1:T(8,128)(2,1)}) %all-gather.5.cloned.1.call-update) | async-done | bytes 1048592 | tf_op jit(solution)/shard_map/all_gather | solution.py:98
  391.2 1.9 copy.19
  393.1 1.1 slice_bitcast_fusion.1
  394.2 3.8 fusion.115
  398.0 0.1 fusion.22
  398.1 1.0 fusion.14
  399.1 0.7 copy.20
  (34 shorter events, 0.2 us)
Async XLA Ops:
  6.5 387.7 %copy-start = (bf16[8192,128]{1,0:T(8,128)(2,1)S(1)}, bf16[8192,128]{1,0:T(8,128)(2,1)}, u32[]{:S(2)}) copy-start(bf16[8192,128]{1,0:T(8,128)(2,1)} %param.28) | copy-start | bytes 6291460
  6.5 5.3 %copy-start.2 = (f32[1280]{0:T(1024)S(1)}, f32[1280]{0:T(1024)}, u32[]{:S(2)}) copy-start(f32[1280]{0:T(1024)} %param.19) | copy-start | bytes 15364
  6.5 5.4 %copy-start.3 = (f32[1280]{0:T(1024)S(1)}, f32[1280]{0:T(1024)}, u32[]{:S(2)}) copy-start(f32[1280]{0:T(1024)} %param.18) | copy-start | bytes 15364
  6.5 5.4 %copy-start.6 = (f32[80]{0:T(128)S(1)}, f32[80]{0:T(128)}, u32[]{:S(2)}) copy-start(f32[80]{0:T(128)} %param.21) | copy-start | bytes 964
  6.5 177.2 %reduce-scatter.2.cloned.1.call-start = ((), (), s32[]{:S(2)}) async-start(), calls=%async_computation.2 | async-start | bytes 1064960 | tf_op jit(solution)/shard_map/reduce_scatter | solution.py:45
  11.6 4.0 copy-start.4
  11.6 172.1 %copy-start.10 = (f32[128]{0:T(128)S(1)}, f32[128]{0:T(128)}, u32[]{:S(2)}) copy-start(f32[128]{0:T(128)} %param.23) | copy-start | bytes 1540
  15.5 287.3 %copy-start.7 = (bf16[8192,2,16]{0,2,1:T(8,128)(2,1)S(1)}, bf16[8192,2,16]{0,2,1:T(8,128)(2,1)}, u32[]{:S(2)}) copy-start(bf16[8192,2,16]{0,2,1:T(8,128)(2,1)} %param.30) | copy-start | bytes 1572868
  15.5 287.3 %copy-start.8 = (f32[8192]{0:T(1024)S(1)}, f32[8192]{0:T(1024)}, u32[]{:S(2)}) copy-start(f32[8192]{0:T(1024)} %param.27) | copy-start | bytes 98308
  185.3 24.2 %all-to-all-start = ((bf16[16,4,128]{2,1,0:T(4,128)(2,1)}), bf16[16,4,128]{2,1,0:T(4,128)(2,1)S(1)}, u32[]{:S(2)}, u32[]{:S(2)}) async-start(bf16[16,4,128]{2,1,0:T(4,128)(2,1)} %bitcast.4), calls=%async_computation.1 | async-start | bytes 32768 | tf_op jit(solution)/shard_map/all_to_all | solution.py:62
  198.1 101.5 %all-gather.3.cloned.1.call-start = ((), (), s32[]{:S(2)}) async-start(), calls=%async_computation.3 | async-start | bytes 4259840 | tf_op jit(solution)/shard_map/all_gather | solution.py:86
  211.9 179.3 %all-gather.5.cloned.1.call-start = ((), (), s32[]{:S(2)}) async-start(), calls=%async_computation.4 | async-start | bytes 1064960 | tf_op jit(solution)/shard_map/all_gather | solution.py:98
  299.5 3.4 copy-start.1
  302.8 1.6 copy-start.5
  303.0 91.2 %copy-start.9 = (s32[1,256]{1,0:T(1,128)S(1)}, s32[1,256]{1,0:T(1,128)}, u32[]{:S(2)}) copy-start(s32[1,256]{1,0:T(1,128)} %param.26) | copy-start | bytes 3076
  303.0 91.2 %copy-start.11 = (f32[128]{0:T(128)S(1)}, f32[128]{0:T(128)}, u32[]{:S(2)}) copy-start(f32[128]{0:T(128)} %param.29) | copy-start | bytes 1540
Sparse Core Ops, SparseCore 0:
  15.6 168.0 reduce-scatter.1
  212.1 87.4 all-gather.2
  305.2 85.9 all-gather.4
where the time goes:
time: 407 us; the launch traced here: 406 us
  waiting for transfers between devices  349 us (86%)
  between operations  13.4 us (3%)
  starting transfers between devices  12.9 us (3%)
  matrix products  11.4 us (3%)
  other arithmetic  11 us (3%)
  local copies, waits for them, and re-layouts  8.42 us (2%)
    reduce_scatter x1, waiting for transfers between devices, per_device(): lax.psum_scatter(partial_sum, 'mp', scatter_dimension=1, tiled=True)  164 us
    all_gather x1, waiting for transfers between devices, per_device(): sequence = lax.all_gather(own_cols, 'mp', axis=1, tiled=True)  87.5 us
    all_gather x1, waiting for transfers between devices, per_device(): keyval_full = lax.all_gather(keyval_local, 'mp', axis=2, tiled=True)  86.1 us
    all_to_all x1, starting transfers between devices, per_device(): lax.all_to_all(outgoing.reshape(owners, capacity, col_width), ('group', '...  12.8 us
    all_to_all x1, waiting for transfers between devices, per_device(): lax.all_to_all(outgoing.reshape(owners, capacity, col_width), ('group', '...  11.3 us
  transfers between devices with their start and end apart: 4, of which 4 were waited for; matrix products, arithmetic and copies ran while one was open for 1% of the time, Pallas kernels for 0%

commit v1 on v0

v1 whole, which is shorter than its diff:
```python
import functools
import math

import jax
import jax.numpy as jnp
from jax import lax
from jax.experimental import pallas as pl
from jax.experimental.pallas import tpu as pltpu
from jax.sharding import PartitionSpec as P

HEADS = 64
KV_HEADS = 8
HEAD_DIM = 128
D = 8192
ROWS = 32
SEQ = 256
NX, NY, NC, NZ = 4, 8, 2, 16
CAP = 4
IMG = NZ * CAP
VIS = 1280
CHUNK = 1024
MESH = pl.DeviceIdType.MESH
BF, F32, I32 = jnp.bfloat16, jnp.float32, jnp.int32

FAR_Y = (4, 3, 5, 2, 6, 1, 7)
NEAR_Y = (1, 7, 2, 6, 3, 5, 4)
FAR_X = (2, 1, 3)
FAR_Z = (8, 7, 9, 6, 10, 5, 11, 4, 12, 3, 13, 2, 14, 1, 15)


def iota(shape, dim):
    return lax.broadcasted_iota(I32, shape, dim)


def onehot(mask):
    return jnp.where(mask, F32(1), F32(0)).astype(BF)


def dot(a, b):
    return jnp.dot(a, b, preferred_element_type=F32)


def dot_nt(a, b):
    return lax.dot_general(a, b, (((1,), (1,)), ((), ())), preferred_element_type=F32)


def kernel(*refs):
    n_in = 15
    ins, out_ref, vin = refs[:n_in], refs[n_in], refs[n_in + 1 : 2 * n_in + 1]
    (ps, cr, xs, xr, os_, ys, yr, zs, zr, gb, k1s, k1, k2, l1s, l1, l2, qt, kvt, sel_s, pls_s, msk_s, merged_s,
     in_sem, snd, cr_sem, xr_sem, yr_sem, zr_sem, gy_sem, gx_sem, gc_sem, k1_sem, k2_sem, l1_sem, l2_sem) = refs[2 * n_in + 1 :]
    (patch, lng, lnb, mut, mub, md, mdb, ro, text, doc, rg, wq, qb, wkv, kvb) = vin

    zhi, zlo, mp = lax.axis_index("group"), lax.axis_index("dp"), lax.axis_index("mp")
    z = zhi * 4 + zlo
    y, x, c = mp // 8, (mp // 2) % 4, mp % 2
    xc = x * 2 + c
    oc = 1 - c

    def at_mp(yy, xx, cc):
        return {"mp": yy * 8 + xx * 2 + cc}

    def at_z(zz):
        return {"group": zz // 4, "dp": zz % 4}

    sibling = at_mp(y, x, oc)
    x_peer = {k: at_mp(y, (x + k) % NX, c) for k in FAR_X}
    y_peer = {k: at_mp((y + k) % NY, x, c) for k in FAR_Y}
    z_peer = {k: at_z((z + k) % NZ) for k in FAR_Z}
    row_peer = {k: at_mp(y, ((xc + k) % 8) // 2, ((xc + k) % 8) % 2) for k in range(1, 8)}

    barrier = pltpu.get_barrier_semaphore()
    others = [sibling] + list(x_peer.values()) + list(y_peer.values()) + list(z_peer.values())
    others += [at_mp(y, (x + k) % NX, oc) for k in FAR_X]
    for peer in others:
        pl.semaphore_signal(barrier, inc=1, device_id=peer, device_id_type=MESH)

    loads = [pltpu.make_async_copy(ins[i], vin[i], in_sem.at[i]) for i in range(n_in)]
    for i in (0, 1, 2, 3, 4, 5, 6, 7, 9, 8, 10, 11, 12, 13, 14):
        loads[i].start()

    sends = []

    def send(src, dst, recv_sem, peer):
        copy = pltpu.make_async_remote_copy(
            src_ref=src, dst_ref=dst, send_sem=snd.at[len(sends)], recv_sem=recv_sem, device_id=peer, device_id_type=MESH
        )
        copy.start()
        sends.append(copy)

    def arrive(ref, sem):
        pltpu.make_async_remote_copy(
            src_ref=ref, dst_ref=ref, send_sem=snd.at[0], recv_sem=sem, device_id=sibling, device_id_type=MESH
        ).wait_recv()

    loads[0].wait()
    order = onehot(iota((128, 128), 1) == (iota((128, 128), 0) % ROWS) * 4 + iota((128, 128), 0) // ROWS)
    pixels = dot(order, patch[...])
    center = pixels - jnp.mean(pixels, axis=-1, keepdims=True)
    spread = jnp.mean(center * center, axis=-1, keepdims=True)
    loads[1].wait()
    loads[2].wait()
    normed = (center * lax.rsqrt(spread + 1e-06) * lng[...][None, :] + lnb[...][None, :]).astype(BF)
    merged_s[...] = normed
    loads[3].wait()
    loads[4].wait()
    up = jnp.zeros((ROWS, 80), F32) + mub[...]
    acc = jnp.zeros((ROWS, 80), F32)
    for p in range(4):
        acc += dot_nt(merged_s[p * ROWS : (p + 1) * ROWS, :], mut[:, p * VIS : (p + 1) * VIS])
    up = acc + up
    hidden = (0.5 * up * (1.0 + lax.erf(up * F32(math.sqrt(0.5))))).astype(BF)
    loads[5].wait()

    def down(i, carry):
        part = dot(hidden, md[:, pl.ds(pl.multiple_of(i * CHUNK, CHUNK), CHUNK)])
        for xx in range(NX):
            for cc in range(NC):
                j = xx * 2 + cc
                ps[cc, xx, i] = part[:, j * 128 : (j + 1) * 128]
        return carry

    lax.fori_loop(0, NY, down, 0)

    pl.semaphore_wait(barrier, len(others))

    for k in FAR_X + (0,):
        slot = (x + k) % NX
        send(ps.at[oc, slot], cr.at[slot], cr_sem.at[slot], sibling)

    loads[7].wait()
    owner = ro[...]
    r_lane = iota((1, 512), 1)
    eq16 = onehot(jnp.broadcast_to(owner, (16, 512)) == iota((16, 512), 0))
    before = onehot((iota((512, 512), 0) < iota((512, 512), 1)) & (iota((512, 512), 0) // ROWS == iota((512, 512), 1) // ROWS))
    earlier = dot(eq16, before)
    block_rank = jnp.sum(earlier * eq16.astype(F32), axis=0, keepdims=True)
    slot_of = owner * 8 + block_rank.astype(I32)
    pick = onehot((jnp.broadcast_to(slot_of, (128, 512)) == iota((128, 512), 0)) & (jnp.broadcast_to(r_lane, (128, 512)) // ROWS == z))
    fold = onehot(iota((512, ROWS), 0) % ROWS == iota((512, ROWS), 1))
    sel_s[...] = dot(pick, fold).astype(BF)
    mine = onehot(jnp.broadcast_to(owner, (16, 512)) == z)
    same = onehot(iota((512, 128), 0) // ROWS == iota((512, 128), 1) // 8)
    ahead = onehot(iota((512, 128), 0) // ROWS < iota((512, 128), 1) // 8)
    count = dot(mine, same)[0:1]
    offset = dot(mine, ahead)[0:1]
    place_k = (iota((1, 128), 1) % 8).astype(F32)
    target = jnp.where(place_k < count, offset + place_k, F32(-1))
    place = jnp.where(jnp.broadcast_to(target, (IMG, 128)) == iota((IMG, 128), 0).astype(F32), F32(1), F32(0))
    pls_s[...] = place.astype(BF)
    msk_s[...] = jnp.broadcast_to(jnp.sum(place, axis=1, keepdims=True), (IMG, 128))

    for k in FAR_X + (0,):
        slot = (x + k) % NX
        arrive(cr.at[slot], cr_sem.at[slot])
        both = ps[c, slot] + cr[slot]
        if k:
            xs[k - 1] = both.astype(BF)
            send(xs.at[k - 1], xr.at[k - 1], xr_sem.at[k - 1], x_peer[k])
        else:
            os_[...] = both

    def project(get):
        def squares(i, total):
            v = get(i).astype(F32)
            v = v * v
            for j in range(CHUNK // 128):
                total = total + v[:, j * 128 : (j + 1) * 128]
            return total

        total = lax.fori_loop(0, D // CHUNK, squares, jnp.zeros((IMG, 128), F32))
        inv = lax.rsqrt(jnp.sum(total, axis=-1, keepdims=True) / D + 1e-06)

        def products(i, carry):
            q, kv = carry
            cols = pl.ds(pl.multiple_of(i * CHUNK, CHUNK), CHUNK)
            n = (get(i).astype(F32) * inv * rg[:, cols]).astype(BF)
            return q + dot(n, wq[cols, :]), kv + dot_nt(n, wkv[:, cols])

        q, kv = lax.fori_loop(0, D // CHUNK, products, (jnp.zeros((IMG, 128), F32), jnp.zeros((IMG, 32), F32)))
        kv_bias = jnp.concatenate([kvb[0:1, :], kvb[1:2, :]], axis=1)
        return (q + qb[...]).astype(BF), (kv + kv_bias).astype(BF)

    def text_rows(r):
        q, kv = project(lambda i: text[r * IMG : (r + 1) * IMG, pl.ds(pl.multiple_of(i * CHUNK, CHUNK), CHUNK)])
        qt[r * IMG : (r + 1) * IMG, :] = q
        kvt[r * IMG : (r + 1) * IMG, :] = kv

    for i in (6, 8, 9, 10, 11, 12, 13, 14):
        loads[i].wait()
    text_rows(0)

    for k in FAR_X:
        arrive(xr.at[k - 1], xr_sem.at[k - 1])
    for k in FAR_Y:
        yy = (y + k) % NY
        tot = os_[yy]
        for j in range(3):
            tot = tot + xr[j, yy].astype(F32)
        ys[k - 1] = tot.astype(BF)
        send(ys.at[k - 1], yr.at[k - 1], yr_sem.at[k - 1], y_peer[k])

    text_rows(1)
    text_rows(2)

    vision = os_[y]
    for j in range(3):
        vision = vision + xr[j, y].astype(F32)
    for k in NEAR_Y:
        arrive(yr.at[k - 1], yr_sem.at[k - 1])
        vision = vision + yr[k - 1].astype(F32)
    vision = (vision + mdb[...]).astype(BF)

    zs[...] = dot(sel_s[...], vision).reshape(NZ, 8, 128).astype(BF)
    for k in FAR_Z:
        send(zs.at[(z + k) % NZ], zr.at[z], zr_sem.at[z], z_peer[k])
    zr[z] = zs[z]

    def pack(kv, halves):
        rows = 4 * halves
        o, i = iota((8 * rows, 32), 0), iota((8 * rows, 32), 1)
        wanted = ((o // 2) % 2) * 16 + (o % 2) * 8 + o // rows
        packed = jnp.zeros((8 * rows, 128), F32)
        for h in range(halves):
            chosen = onehot((i == wanted) & ((o % rows) // 4 == h))
            packed += dot_nt(chosen, kv[h * 128 : (h + 1) * 128, :])
        return packed.reshape(8, rows, 128).astype(BF)

    def head_of(held, h, t):
        rows = held.shape[2]
        r, dd = iota((128, 64 * rows), 1), iota((128, 64 * rows), 0)
        source = ((r // rows) % 8) * 16 + (r // (8 * rows)) * 2 + r % 2
        chosen = onehot((dd == source) & ((r % rows) // 2 == h * 2 + t))
        flat = held[...].astype(F32).reshape(64 * rows, 128).astype(BF)
        return dot(chosen, flat).astype(BF)

    def spread_y(src, dst, sems):
        for k in FAR_Y:
            send(src.at[(y + k) % NY], dst.at[y], sems.at[y], y_peer[k])
        dst[y] = src[y]

    def gather_y(dst, sems):
        for k in NEAR_Y:
            yy = (y + k) % NY
            arrive(dst.at[yy], sems.at[yy])

    def spread_row(src, dst, sems):
        for k in (4, 3, 5, 2, 6, 1, 7):
            send(src, dst.at[xc], sems.at[xc], row_peer[k])
        dst[xc] = src[...]

    def gather_row(dst, sems):
        for k in range(1, 8):
            j = (xc + k) % 8
            arrive(dst.at[j], sems.at[j])

    text_rows(3)
    k1s[...] = pack(kvt[...], 2)
    spread_y(k1s, k1, k1_sem)

    for k in range(1, NZ):
        zz = (z + k) % NZ
        arrive(zr.at[zz], zr_sem.at[zz])
    arrived = zr[...].astype(F32).reshape(NZ * 8, 128).astype(BF)
    placed = dot(pls_s[...], arrived)
    own_text = text[0:IMG, pl.ds(pl.multiple_of(mp * 128, 128), 128)].astype(F32)
    gb[c, x, y] = jnp.where(msk_s[...] > 0.5, placed, own_text).astype(BF)

    def block(xx, k):
        return gb.at[c, xx % NX, (y + k) % NY]

    def share_x(k):
        for kk in (1, 3):
            send(block(x, k), block(x, k), gx_sem.at[x, (y + k) % NY], x_peer[kk])

    def relay_x(j, k):
        frm, to = (3, 1) if j % 2 == 0 else (1, 3)
        src = (x + frm) % NX
        arrive(block(src, k), gx_sem.at[src, (y + k) % NY])
        send(block(src, k), block(src, k), gx_sem.at[src, (y + k) % NY], x_peer[to])

    for k in FAR_Y:
        send(block(x, 0), block(x, 0), gy_sem.at[y], y_peer[k])
    order_y = (0,) + NEAR_Y
    for j, k in enumerate(order_y):
        if k:
            arrive(block(x, k), gy_sem.at[(y + k) % NY])
        share_x(k)
        if j >= 2:
            relay_x(j - 2, order_y[j - 2])
    send(gb.at[c, x], gb.at[c, x], gc_sem.at[x], sibling)
    for j in (6, 7):
        relay_x(j, order_y[j])
    for kk in (1, 3, 2):
        xx = (x + kk) % NX
        for j, k in enumerate(order_y):
            if kk == 2 or j % 2 == (kk == 1):
                continue
            arrive(block(xx, k), gx_sem.at[xx, (y + k) % NY])
        if kk == 2:
            for k in order_y:
                arrive(block(xx, k), gx_sem.at[xx, (y + k) % NY])
        send(gb.at[c, xx], gb.at[c, xx], gc_sem.at[xx], sibling)
    gather_y(k1, k1_sem)
    spread_row(k1, k2, k2_sem)
    for k in (0, 1, 3, 2):
        xx = (x + k) % NX
        arrive(gb.at[oc, xx], gc_sem.at[xx])

    q_late, kv_late = project(
        lambda i: jnp.concatenate([gb[cc, xx, i] for xx in range(NX) for cc in range(NC)], axis=1)
    )
    l1s[...] = pack(jnp.concatenate([kv_late, kvt[IMG:128, :]], axis=0), 1)
    spread_y(l1s, l1, l1_sem)

    docs = doc[...].astype(F32)

    def attend(q, keys, values, q0, k0):
        n, m = q.shape[0], keys.shape[1]
        s = dot(q, keys) / math.sqrt(HEAD_DIM)
        row, col = iota((n, m), 0) + q0, iota((n, m), 1) + k0
        eye = jnp.where(iota((n, n), 0) == iota((n, n), 1), docs[:, q0 : q0 + n], F32(0))
        doc_q = jnp.sum(eye, axis=1, keepdims=True)
        s = jnp.where((doc_q == docs[:, k0 : k0 + m]) & (col <= row), s, F32(-1e30))
        w = jnp.exp(s - jnp.max(s, axis=-1, keepdims=True))
        p = (w / jnp.sum(w, axis=-1, keepdims=True)).astype(BF)
        return dot_nt(p, values).astype(BF)

    gather_row(k2, k2_sem)
    keys = jnp.concatenate([head_of(k2, h, 0) for h in range(2)], axis=1)
    values = jnp.concatenate([head_of(k2, h, 1) for h in range(2)], axis=1)
    out_ref[128:256, :] = attend(qt[128:256, :], keys, values, 128, 0)

    gather_y(l1, l1_sem)
    spread_row(l1, l2, l2_sem)
    gather_row(l2, l2_sem)
    q_first = jnp.concatenate([q_late, qt[IMG:128, :]], axis=0)
    out_ref[0:128, :] = attend(q_first, head_of(l2, 0, 0), head_of(l2, 0, 1), 0, 0)

    for copy in sends:
        copy.wait_send()


def per_device(patch_rows, ln_gain, ln_bias, merge_up, merge_up_bias, merge_down, merge_down_bias, row_owner,
               text_embed, doc_ids, rms_gain, w_query, query_bias, w_keyval, keyval_bias):
    args = (
        patch_rows.reshape(128, VIS),
        ln_gain,
        ln_bias,
        merge_up.T,
        merge_up_bias.reshape(1, 80),
        merge_down,
        merge_down_bias.reshape(1, 128),
        row_owner.reshape(1, 512),
        text_embed.reshape(SEQ, D),
        doc_ids,
        rms_gain.reshape(1, D),
        w_query,
        query_bias.reshape(1, 128),
        jnp.transpose(w_keyval, (1, 2, 0)).reshape(32, D),
        keyval_bias,
    )
    dma = pltpu.SemaphoreType.DMA
    n_sends = 4 + 3 + 7 + 15 + 7 + 7 + 7 + 24 + 4 + 7 + 7
    scratch = [pltpu.VMEM(a.shape, a.dtype) for a in args]
    scratch += [
        pltpu.VMEM((NC, NX, NY, ROWS, 128), F32),
        pltpu.VMEM((NX, NY, ROWS, 128), F32),
        pltpu.VMEM((3, NY, ROWS, 128), BF),
        pltpu.VMEM((3, NY, ROWS, 128), BF),
        pltpu.VMEM((NY, ROWS, 128), F32),
        pltpu.VMEM((7, ROWS, 128), BF),
        pltpu.VMEM((7, ROWS, 128), BF),
        pltpu.VMEM((NZ, 8, 128), BF),
        pltpu.VMEM((NZ, 8, 128), BF),
        pltpu.VMEM((NC, NX, NY, IMG, 128), BF),
        pltpu.VMEM((8, 8, 128), BF),
        pltpu.VMEM((8, 8, 128), BF),
        pltpu.VMEM((8, 8, 8, 128), BF),
        pltpu.VMEM((8, 4, 128), BF),
        pltpu.VMEM((8, 4, 128), BF),
        pltpu.VMEM((8, 8, 4, 128), BF),
        pltpu.VMEM((SEQ, 128), BF),
        pltpu.VMEM((SEQ, 32), BF),
        pltpu.VMEM((128, ROWS), BF),
        pltpu.VMEM((IMG, 128), BF),
        pltpu.VMEM((IMG, 128), F32),
        pltpu.VMEM((128, VIS), BF),
        dma((len(args),)),
        dma((n_sends,)),
        dma((4,)), dma((3,)), dma((7,)), dma((16,)), dma((8,)), dma((4, 8)), dma((4,)),
        dma((8,)), dma((8,)), dma((8,)), dma((8,)),
    ]
    out = pl.pallas_call(
        kernel,
        out_shape=jax.ShapeDtypeStruct((SEQ, 128), BF),
        in_specs=[pl.BlockSpec(memory_space=pl.ANY)] * len(args),
        out_specs=pl.BlockSpec(memory_space=pltpu.VMEM),
        scratch_shapes=scratch,
        compiler_params=pltpu.CompilerParams(
            collective_id=0, has_side_effects=True, vmem_limit_bytes=67043328
        ),
        name="step",
    )(*args)
    return out.reshape(1, SEQ, 128)


def solution(mesh):
    in_specs = (
        P(("group", "dp"), None, None),
        P(None),
        P(None),
        P(None, "mp"),
        P("mp"),
        P("mp", None),
        P("mp"),
        P(None, None),
        P(("group", "dp"), None, None),
        P(("group", "dp"), None),
        P(None),
        P(None, "mp"),
        P("mp"),
        P(None, None, "mp"),
        P(None, "mp"),
    )
    return jax.shard_map(
        per_device,
        mesh=mesh,
        in_specs=in_specs,
        out_specs=P(("group", "dp"), None, "mp"),
        check_vma=False,
    )
```

time: 407 us -> 75.8 us (0.19)
  waiting for transfers between devices: 349 us -> 0 us
  Pallas kernels: 0 us -> 74.2 us
  between operations: 13.4 us -> 0.01 us
  starting transfers between devices: 12.9 us -> 0 us
  matrix products: 11.4 us -> 0 us
  other arithmetic: 11 us -> 0 us
  local copies, waits for them, and re-layouts: 8.42 us -> 1.47 us
    all_gather x2 -> x0, waiting for transfers between devices: 174 us -> none  [the longest x1 87.5 us: per_device(): sequence = lax.all_gather(own_cols, 'mp', axis=1, tiled=True)]
    reduce_scatter x1 -> x0, waiting for transfers between devices: 164 us -> none  [per_device(): lax.psum_scatter(partial_sum, 'mp', scatter_dimension=1, tiled=True)]
    pallas_call x0 -> x1, Pallas kernels: none -> 74.2 us  [per_device(): pl.pallas_call(kernel, out_shape=jax.ShapeDtypeStruct((SEQ, 128), BF), in...]
    all_to_all x1 -> x0, starting transfers between devices: 12.8 us -> none  [per_device(): lax.all_to_all(outgoing.reshape(owners, capacity, col_width), ('group', '...]
    all_to_all x1 -> x0, waiting for transfers between devices: 11.3 us -> none  [per_device(): lax.all_to_all(outgoing.reshape(owners, capacity, col_width), ('group', '...]
    dot_general x4 -> x0, matrix products: 9.99 us -> none  [the longest x1 3.83 us: per_device(): jnp.einsum('qhd,khd->hqk', query_heads, keys, preferred_element_type=jnp....]
    reduce_sum x8 -> x0, other arithmetic: 7.14 us -> none  [the longest x1 3.25 us: per_device(): jnp.mean(seq_f * seq_f, axis=-1, keepdims=True) + 1e-06]
  transfers between devices with their start and end apart: 4 -> 0, of which waited for: 4 -> 0; matrix products, arithmetic and copies ran while one was open for 1% -> 0% of each run, Pallas kernels for 0% -> 0%
where the time goes in v1:
time: 75.8 us; the launch traced here: 75.7 us
  Pallas kernels  74.2 us (98%)
  local copies, waits for them, and re-layouts  1.47 us (2%)
    pallas_call x1, Pallas kernels, per_device(): pl.pallas_call(kernel, out_shape=jax.ShapeDtypeStruct((SEQ, 128), BF), in...  74.2 us

profile of v1, /device:TPU:1, one launch (start us, length us, event | category | flops | bytes accessed | tf_op | source)
XLA Modules:
  0.0 75.7 jit_solution(4726337437733525709)
XLA Ops:
  0.0 74.2 %step.1 = bf16[256,128]{1,0:T(8,128)(2,1)} custom-call(bf16[128,1280]{1,0:T(8,128)(2,1)} %bitcast.15, f32[1280]{0:T(1024)} %refs_1_.1, f32[1280]{0:T(1024)} %refs_2_.1, bf16[80,5120]{1,0:T(8,128)(2,1)} %bitcast.13, f32[1,80]{1,0:T(1,128)} %bitcast.19, bf16[80,8192]{1,0:T(8,128)(2,1)} %refs_5_.1, f32[1,128]{1,0:T(1,128)} %bitcast.20, s32[1,512]{1,0:T(1,128)} %bitcast.18, ...), custom_call_target="tpu_custom_call" | custom-call | tf_op jit(solution)/shard_map/step/pallas_call | solution.py:394
  74.2 1.5 %copy.17 = bf16[1,256,128]{2,1,0:T(8,128)(2,1)} copy(bf16[1,256,128]{2,1,0:T(8,128)(2,1)} %bitcast.16) | data formatting | bytes 131072

commit v2 on v1

--- a/solution.py
+++ b/solution.py
@@ -47,7 +47,7 @@
 def kernel(*refs):
     n_in = 15
     ins, out_ref, vin = refs[:n_in], refs[n_in], refs[n_in + 1 : 2 * n_in + 1]
-    (ps, cr, xs, xr, os_, ys, yr, zs, zr, gb, k1s, k1, k2, l1s, l1, l2, qt, kvt, sel_s, pls_s, msk_s, merged_s,
+    (ps, cr, xs, xr, os_, ys, yr, zs, zr, gb, k1s, k1, k2, l1s, l1, l1c, l2, qt, kvt, sel_s, pls_s, msk_s, merged_s,
      in_sem, snd, cr_sem, xr_sem, yr_sem, zr_sem, gy_sem, gx_sem, gc_sem, k1_sem, k2_sem, l1_sem, l2_sem) = refs[2 * n_in + 1 :]
     (patch, lng, lnb, mut, mub, md, mdb, ro, text, doc, rg, wq, qb, wkv, kvb) = vin
 
@@ -217,21 +217,21 @@
     zr[z] = zs[z]
 
     def pack(kv, halves):
-        rows = 4 * halves
-        o, i = iota((8 * rows, 32), 0), iota((8 * rows, 32), 1)
-        wanted = ((o // 2) % 2) * 16 + (o % 2) * 8 + o // rows
-        packed = jnp.zeros((8 * rows, 128), F32)
+        o, i = iota((64, 32), 0), iota((64, 32), 1)
+        wanted = ((o // 2) % 2) * 16 + (o % 2) * 8 + o // 8
+        packed = jnp.zeros((64, 128), F32)
         for h in range(halves):
-            chosen = onehot((i == wanted) & ((o % rows) // 4 == h))
+            chosen = onehot((i == wanted) & ((o // 4) % 2 == h))
             packed += dot_nt(chosen, kv[h * 128 : (h + 1) * 128, :])
-        return packed.reshape(8, rows, 128).astype(BF)
-
-    def head_of(held, h, t):
-        rows = held.shape[2]
+        return packed.reshape(8, 8, 128).astype(BF)
+
+    def flat_of(held):
+        return held[...].astype(F32).reshape(-1, 128).astype(BF)
+
+    def head_of(flat, rows, h, t):
         r, dd = iota((128, 64 * rows), 1), iota((128, 64 * rows), 0)
         source = ((r // rows) % 8) * 16 + (r // (8 * rows)) * 2 + r % 2
         chosen = onehot((dd == source) & ((r % rows) // 2 == h * 2 + t))
-        flat = held[...].astype(F32).reshape(64 * rows, 128).astype(BF)
         return dot(chosen, flat).astype(BF)
 
     def spread_y(src, dst, sems):
@@ -257,6 +257,8 @@
     text_rows(3)
     k1s[...] = pack(kvt[...], 2)
     spread_y(k1s, k1, k1_sem)
+    gather_y(k1, k1_sem)
+    spread_row(k1, k2, k2_sem)
 
     for k in range(1, NZ):
         zz = (z + k) % NZ
@@ -269,40 +271,26 @@
     def block(xx, k):
         return gb.at[c, xx % NX, (y + k) % NY]
 
-    def share_x(k):
-        for kk in (1, 3):
-            send(block(x, k), block(x, k), gx_sem.at[x, (y + k) % NY], x_peer[kk])
-
-    def relay_x(j, k):
-        frm, to = (3, 1) if j % 2 == 0 else (1, 3)
-        src = (x + frm) % NX
-        arrive(block(src, k), gx_sem.at[src, (y + k) % NY])
-        send(block(src, k), block(src, k), gx_sem.at[src, (y + k) % NY], x_peer[to])
-
+    order_y = (0,) + NEAR_Y
+    early = order_y[:4]
     for k in FAR_Y:
         send(block(x, 0), block(x, 0), gy_sem.at[y], y_peer[k])
-    order_y = (0,) + NEAR_Y
-    for j, k in enumerate(order_y):
+    for k in order_y:
         if k:
             arrive(block(x, k), gy_sem.at[(y + k) % NY])
-        share_x(k)
-        if j >= 2:
-            relay_x(j - 2, order_y[j - 2])
+        for kk in (1, 3) if k in early else FAR_X:
+            send(block(x, k), block(x, k), gx_sem.at[x, (y + k) % NY], x_peer[kk])
+    nxt = (x + 1) % NX
+    for k in early:
+        arrive(block(nxt, k), gx_sem.at[nxt, (y + k) % NY])
+        send(block(nxt, k), block(nxt, k), gx_sem.at[nxt, (y + k) % NY], x_peer[3])
     send(gb.at[c, x], gb.at[c, x], gc_sem.at[x], sibling)
-    for j in (6, 7):
-        relay_x(j, order_y[j])
     for kk in (1, 3, 2):
         xx = (x + kk) % NX
-        for j, k in enumerate(order_y):
-            if kk == 2 or j % 2 == (kk == 1):
-                continue
-            arrive(block(xx, k), gx_sem.at[xx, (y + k) % NY])
-        if kk == 2:
-            for k in order_y:
+        for k in order_y:
+            if kk != 1 or k not in early:
                 arrive(block(xx, k), gx_sem.at[xx, (y + k) % NY])
         send(gb.at[c, xx], gb.at[c, xx], gc_sem.at[xx], sibling)
-    gather_y(k1, k1_sem)
-    spread_row(k1, k2, k2_sem)
     for k in (0, 1, 3, 2):
         xx = (x + k) % NX
         arrive(gb.at[oc, xx], gc_sem.at[xx])
@@ -327,15 +315,19 @@
         return dot_nt(p, values).astype(BF)
 
     gather_row(k2, k2_sem)
-    keys = jnp.concatenate([head_of(k2, h, 0) for h in range(2)], axis=1)
-    values = jnp.concatenate([head_of(k2, h, 1) for h in range(2)], axis=1)
+    flat = flat_of(k2)
+    keys = jnp.concatenate([head_of(flat, 8, h, 0) for h in range(2)], axis=1)
+    values = jnp.concatenate([head_of(flat, 8, h, 1) for h in range(2)], axis=1)
     out_ref[128:256, :] = attend(qt[128:256, :], keys, values, 128, 0)
 
     gather_y(l1, l1_sem)
-    spread_row(l1, l2, l2_sem)
+    used = (iota((32, 64), 0) // 4) * 8 + iota((32, 64), 0) % 4
+    l1c[...] = dot(onehot(iota((32, 64), 1) == used), flat_of(l1)).reshape(4, 8, 128).astype(BF)
+    spread_row(l1c, l2, l2_sem)
     gather_row(l2, l2_sem)
     q_first = jnp.concatenate([q_late, qt[IMG:128, :]], axis=0)
-    out_ref[0:128, :] = attend(q_first, head_of(l2, 0, 0), head_of(l2, 0, 1), 0, 0)
+    flat = flat_of(l2)
+    out_ref[0:128, :] = attend(q_first, head_of(flat, 4, 0, 0), head_of(flat, 4, 0, 1), 0, 0)
 
     for copy in sends:
         copy.wait_send()
@@ -377,9 +369,10 @@
         pltpu.VMEM((8, 8, 128), BF),
         pltpu.VMEM((8, 8, 128), BF),
         pltpu.VMEM((8, 8, 8, 128), BF),
-        pltpu.VMEM((8, 4, 128), BF),
-        pltpu.VMEM((8, 4, 128), BF),
-        pltpu.VMEM((8, 8, 4, 128), BF),
+        pltpu.VMEM((8, 8, 128), BF),
+        pltpu.VMEM((8, 8, 128), BF),
+        pltpu.VMEM((4, 8, 128), BF),
+        pltpu.VMEM((8, 4, 8, 128), BF),
         pltpu.VMEM((SEQ, 128), BF),
         pltpu.VMEM((SEQ, 32), BF),
         pltpu.VMEM((128, ROWS), BF),

time: 75.8 us -> 69.9 us (0.922)
  Pallas kernels: 74.2 us -> 68.2 us
    pallas_call x1, Pallas kernels: 74.2 us -> 68.2 us  [per_device(): pl.pallas_call(kernel, out_shape=jax.ShapeDtypeStruct((SEQ, 128), BF), in...]
where the time goes in v2:
time: 69.9 us; the launch traced here: 69.7 us
  Pallas kernels  68.2 us (98%)
  local copies, waits for them, and re-layouts  1.47 us (2%)
    pallas_call x1, Pallas kernels, per_device(): pl.pallas_call(kernel, out_shape=jax.ShapeDtypeStruct((SEQ, 128), BF), in...  68.2 us
    unnamed x1, local copies, waits for them, and re-layouts  1.47 us

profile of v2, /device:TPU:1, one launch (start us, length us, event | category | flops | bytes accessed | tf_op | source)
XLA Modules:
  0.0 69.7 jit_solution(10115416804937422559)
XLA Ops:
  0.0 68.2 %step.1 = bf16[256,128]{1,0:T(8,128)(2,1)} custom-call(bf16[128,1280]{1,0:T(8,128)(2,1)} %bitcast.15, f32[1280]{0:T(1024)} %refs_1_.1, f32[1280]{0:T(1024)} %refs_2_.1, bf16[80,5120]{1,0:T(8,128)(2,1)} %bitcast.13, f32[1,80]{1,0:T(1,128)} %bitcast.19, bf16[80,8192]{1,0:T(8,128)(2,1)} %refs_5_.1, f32[1,128]{1,0:T(1,128)} %bitcast.20, s32[1,512]{1,0:T(1,128)} %bitcast.18, ...), custom_call_target="tpu_custom_call" | custom-call | tf_op jit(solution)/shard_map/step/pallas_call | solution.py:387
  68.2 1.5 %copy.17 = bf16[1,256,128]{2,1,0:T(8,128)(2,1)} copy(bf16[1,256,128]{2,1,0:T(8,128)(2,1)} %bitcast.16) | data formatting | bytes 131072

commit v3 on v2

--- a/solution.py
+++ b/solution.py
@@ -48,7 +48,7 @@
     n_in = 15
     ins, out_ref, vin = refs[:n_in], refs[n_in], refs[n_in + 1 : 2 * n_in + 1]
     (ps, cr, xs, xr, os_, ys, yr, zs, zr, gb, k1s, k1, k2, l1s, l1, l1c, l2, qt, kvt, sel_s, pls_s, msk_s, merged_s,
-     in_sem, snd, cr_sem, xr_sem, yr_sem, zr_sem, gy_sem, gx_sem, gc_sem, k1_sem, k2_sem, l1_sem, l2_sem) = refs[2 * n_in + 1 :]
+     in_sem, snd, cr_sem, xr_sem, yr_sem, zr_sem, gy_sem, gx_sem, gc_sem, k1_sem, k2_sem, l1_sem, l2_sem, near_sem) = refs[2 * n_in + 1 :]
     (patch, lng, lnb, mut, mub, md, mdb, ro, text, doc, rg, wq, qb, wkv, kvb) = vin
 
     zhi, zlo, mp = lax.axis_index("group"), lax.axis_index("dp"), lax.axis_index("mp")
@@ -70,7 +70,7 @@
     row_peer = {k: at_mp(y, ((xc + k) % 8) // 2, ((xc + k) % 8) % 2) for k in range(1, 8)}
 
     barrier = pltpu.get_barrier_semaphore()
-    others = [sibling] + list(x_peer.values()) + list(y_peer.values()) + list(z_peer.values())
+    others = [sibling] + list(x_peer.values()) + list(y_peer.values()) + [z_peer[1], z_peer[15]]
     others += [at_mp(y, (x + k) % NX, oc) for k in FAR_X]
     for peer in others:
         pl.semaphore_signal(barrier, inc=1, device_id=peer, device_id_type=MESH)
@@ -120,13 +120,25 @@
                 ps[cc, xx, i] = part[:, j * 128 : (j + 1) * 128]
         return carry
 
-    lax.fori_loop(0, NY, down, 0)
+    lax.fori_loop(0, NY, down, 0, unroll=True)
 
     pl.semaphore_wait(barrier, len(others))
+
+    def greet(r):
+        for k in (1 << r, NZ - (1 << r)):
+            pl.semaphore_signal(near_sem.at[r], inc=1, device_id=z_peer[k], device_id_type=MESH)
+
+    def met(r):
+        pl.semaphore_wait(near_sem.at[r], 2)
+
+    greet(0)
 
     for k in FAR_X + (0,):
         slot = (x + k) % NX
         send(ps.at[oc, slot], cr.at[slot], cr_sem.at[slot], sibling)
+
+    met(0)
+    greet(1)
 
     loads[7].wait()
     owner = ro[...]
@@ -160,7 +172,7 @@
         else:
             os_[...] = both
 
-    def project(get):
+    def project(get, total=None):
         def squares(i, total):
             v = get(i).astype(F32)
             v = v * v
@@ -168,7 +180,8 @@
                 total = total + v[:, j * 128 : (j + 1) * 128]
             return total
 
-        total = lax.fori_loop(0, D // CHUNK, squares, jnp.zeros((IMG, 128), F32))
+        if total is None:
+            total = lax.fori_loop(0, D // CHUNK, squares, jnp.zeros((IMG, 128), F32), unroll=True)
         inv = lax.rsqrt(jnp.sum(total, axis=-1, keepdims=True) / D + 1e-06)
 
         def products(i, carry):
@@ -177,7 +190,7 @@
             n = (get(i).astype(F32) * inv * rg[:, cols]).astype(BF)
             return q + dot(n, wq[cols, :]), kv + dot_nt(n, wkv[:, cols])
 
-        q, kv = lax.fori_loop(0, D // CHUNK, products, (jnp.zeros((IMG, 128), F32), jnp.zeros((IMG, 32), F32)))
+        q, kv = lax.fori_loop(0, D // CHUNK, products, (jnp.zeros((IMG, 128), F32), jnp.zeros((IMG, 32), F32)), unroll=True)
         kv_bias = jnp.concatenate([kvb[0:1, :], kvb[1:2, :]], axis=1)
         return (q + qb[...]).astype(BF), (kv + kv_bias).astype(BF)
 
@@ -189,6 +202,8 @@
     for i in (6, 8, 9, 10, 11, 12, 13, 14):
         loads[i].wait()
     text_rows(0)
+    met(1)
+    greet(2)
 
     for k in FAR_X:
         arrive(xr.at[k - 1], xr_sem.at[k - 1])
@@ -210,6 +225,8 @@
         arrive(yr.at[k - 1], yr_sem.at[k - 1])
         vision = vision + yr[k - 1].astype(F32)
     vision = (vision + mdb[...]).astype(BF)
+
+    met(2)
 
     zs[...] = dot(sel_s[...], vision).reshape(NZ, 8, 128).astype(BF)
     for k in FAR_Z:
@@ -285,18 +302,28 @@
         arrive(block(nxt, k), gx_sem.at[nxt, (y + k) % NY])
         send(block(nxt, k), block(nxt, k), gx_sem.at[nxt, (y + k) % NY], x_peer[3])
     send(gb.at[c, x], gb.at[c, x], gc_sem.at[x], sibling)
+
+    def squares_of(total, cc, xx):
+        for i in range(NY):
+            v = gb[cc, xx, i].astype(F32)
+            total = total + v * v
+        return total
+
+    total = squares_of(jnp.zeros((IMG, 128), F32), c, x)
     for kk in (1, 3, 2):
         xx = (x + kk) % NX
         for k in order_y:
             if kk != 1 or k not in early:
                 arrive(block(xx, k), gx_sem.at[xx, (y + k) % NY])
         send(gb.at[c, xx], gb.at[c, xx], gc_sem.at[xx], sibling)
+        total = squares_of(total, c, xx)
     for k in (0, 1, 3, 2):
         xx = (x + k) % NX
         arrive(gb.at[oc, xx], gc_sem.at[xx])
+        total = squares_of(total, oc, xx)
 
     q_late, kv_late = project(
-        lambda i: jnp.concatenate([gb[cc, xx, i] for xx in range(NX) for cc in range(NC)], axis=1)
+        lambda i: jnp.concatenate([gb[cc, xx, i] for xx in range(NX) for cc in range(NC)], axis=1), total
     )
     l1s[...] = pack(jnp.concatenate([kv_late, kvt[IMG:128, :]], axis=0), 1)
     spread_y(l1s, l1, l1_sem)
@@ -383,6 +410,7 @@
         dma((n_sends,)),
         dma((4,)), dma((3,)), dma((7,)), dma((16,)), dma((8,)), dma((4, 8)), dma((4,)),
         dma((8,)), dma((8,)), dma((8,)), dma((8,)),
+        pltpu.SemaphoreType.REGULAR((3,)),
     ]
     out = pl.pallas_call(
         kernel,

time: 69.9 us -> 65.6 us (0.938)
  Pallas kernels: 68.2 us -> 63.9 us
    pallas_call x1, Pallas kernels: 68.2 us -> 63.9 us  [per_device(): pl.pallas_call(kernel, out_shape=jax.ShapeDtypeStruct((SEQ, 128), BF), in...]
where the time goes in v3:
time: 65.6 us; the launch traced here: 65.4 us
  Pallas kernels  63.9 us (97%)
  local copies, waits for them, and re-layouts  1.47 us (2%)
    pallas_call x1, Pallas kernels, per_device(): pl.pallas_call(kernel, out_shape=jax.ShapeDtypeStruct((SEQ, 128), BF), in...  63.9 us
    unnamed x1, local copies, waits for them, and re-layouts  1.47 us

profile of v3, /device:TPU:1, one launch (start us, length us, event | category | flops | bytes accessed | tf_op | source)
XLA Modules:
  0.0 65.4 jit_solution(17629317464097571351)
XLA Ops:
  0.0 63.9 %step.1 = bf16[256,128]{1,0:T(8,128)(2,1)} custom-call(bf16[128,1280]{1,0:T(8,128)(2,1)} %bitcast.15, f32[1280]{0:T(1024)} %refs_1_.1, f32[1280]{0:T(1024)} %refs_2_.1, bf16[80,5120]{1,0:T(8,128)(2,1)} %bitcast.13, f32[1,80]{1,0:T(1,128)} %bitcast.19, bf16[80,8192]{1,0:T(8,128)(2,1)} %refs_5_.1, f32[1,128]{1,0:T(1,128)} %bitcast.20, s32[1,512]{1,0:T(1,128)} %bitcast.18, ...), custom_call_target="tpu_custom_call" | custom-call | tf_op jit(solution)/shard_map/step/pallas_call | solution.py:415
  63.9 1.5 %copy.17 = bf16[1,256,128]{2,1,0:T(8,128)(2,1)} copy(bf16[1,256,128]{2,1,0:T(8,128)(2,1)} %bitcast.16) | data formatting | bytes 131072
